TPU v7x, 32 devices: a whole 2x2x4 slice. The times are simulated.
32 devices in a mesh: dp: 16 (over z, x, core), tensor: 2 (over y).
Axes of the slice: x: 2, y: 2, z: 4, core: 2. Of those that a mesh axis runs over, the one named last changes fastest.
Arguments:
- inputs: bfloat16 [2048, 2048], P('dp'), may hold values from -6 to 6
- segments: int32 [2048], P('dp'), may hold values from 0 to 1, as said below
- positions: int32 [2048], P('dp'), may hold values from 0 to 1999, as said below
- w_query: bfloat16 [2048, 2048], P('dp', 'tensor')
- w_key: bfloat16 [2048, 512], P('dp', 'tensor')
- w_value: bfloat16 [2048, 512], P('dp', 'tensor'), may hold values from -0.125 to 0.125
- w_out: bfloat16 [2048, 2048], P('dp', 'tensor'), may hold values from -0.5 to 0.5
- w_gate: bfloat16 [2048, 8192], P('dp', 'tensor'), may hold values from -0.125 to 0.125
- w_up: bfloat16 [2048, 8192], P('dp', 'tensor'), may hold values from -0.125 to 0.125
- w_down: bfloat16 [2048, 8192], P('dp', 'tensor'), may hold values from -0.125 to 0.125
- attn_gain: bfloat16 [2048], P('dp'), may hold values from 0.5 to 1.5
- mlp_gain: bfloat16 [2048], P('dp'), may hold values from 0.5 to 1.5
- out_grad: bfloat16 [2048, 2048], P('dp'), may hold values from -6 to 6
Outputs:
- output: bfloat16 [2048, 2048], P('dp')
- input_grad: float32 [2048, 2048], P('dp')
- query_grad: float32 [2048, 2048], P('dp', 'tensor')
- key_grad: float32 [2048, 512], P('dp', 'tensor')
- value_grad: float32 [2048, 512], P('dp', 'tensor')
- out_proj_grad: float32 [2048, 2048], P('dp', 'tensor')
- gate_grad: float32 [2048, 8192], P('dp', 'tensor')
- up_grad: float32 [2048, 8192], P('dp', 'tensor')
- down_grad: float32 [2048, 8192], P('dp', 'tensor')
- attn_gain_grad: float32 [2048], P('dp')
- mlp_gain_grad: float32 [2048], P('dp')
Inputs may be any that keep to these rules, and one draw needn't show every extreme that they name: `segments`: within each sequence of 128 tokens segment numbers start at 0 and rise by one where a document begins; documents span 200 to 2000 tokens of the packed stream, so a sequence's first document may have begun in the sequence before it. `positions`: A token's position within its document: it rises by one from token to token of a document and is 0 where a document begins; at a sequence's first token it continues a document that began earlier.
All inputs are finite; a program needn't handle non-finite values.
Results may differ from a plain program's by a relative error of at most 0.019.
The roundings to bfloat16 on the way count: a program that leaves them out, or rounds other values in their place, can miss the bound.
Values may be sent and summed in bfloat16 or wider, within the bound.
No kernel may reach another device: no remote copies, remote signals or barrier semaphores. Data moves between devices by JAX's collectives and lax.ppermute only.
A program may use at most 256 MiB of HBM per device.

v0:
```python
import math
import jax
import jax.numpy as jnp
from jax import lax
from jax.sharding import PartitionSpec as P

HEADS = 32
KV_HEADS = 8
HEAD_DIM = 64
norm_eps = 1e-05
rope_base = 500000.0
masked_score = -1e30


def rope_freqs(head_dim):
    index = jnp.arange(head_dim // 2, dtype=jnp.float32)
    inverse = rope_base ** (-2.0 * index / head_dim)
    wavelen = 2.0 * math.pi / inverse
    smooth = (8192.0 / wavelen - 1.0) / 3.0
    scaled = (1.0 - smooth) * inverse / 32.0 + smooth * inverse
    return jnp.where(wavelen < 2048.0, inverse, jnp.where(wavelen > 8192.0, inverse / 32.0, scaled))


def rotate(values, cosine, sine):
    half = values.shape[-1] // 2
    first = values[..., :half]
    second = values[..., half:]
    return jnp.concatenate(
        [first * cosine - second * sine, second * cosine + first * sine], axis=-1
    )


def norm_parts(values):
    scale = lax.rsqrt(jnp.mean(values * values, axis=-1, keepdims=True) + norm_eps)
    return (values * scale, scale)


def norm_back(grad, unit, scale, gain):
    weighted = grad * gain
    return (
        scale * (weighted - unit * jnp.mean(weighted * unit, axis=-1, keepdims=True)),
        jnp.sum(grad * unit, axis=0),
    )


def dot_last(left, right):
    return lax.dot_general(
        left, right, (((1,), (1,)), ((), ())), preferred_element_type=jnp.float32
    )


def dot_first(left, right):
    return lax.dot_general(
        left, right, (((0,), (0,)), ((), ())), preferred_element_type=jnp.float32
    )


def on_device(
    inputs,
    segments,
    positions,
    w_query,
    w_key,
    w_value,
    w_out,
    w_gate,
    w_up,
    w_down,
    attn_gain,
    mlp_gain,
    out_grad,
):
    length = inputs.shape[0]
    group = HEADS // KV_HEADS
    factor = HEAD_DIM ** (-0.5)
    residual = inputs.astype(jnp.float32)
    angle = positions.astype(jnp.float32)[:, None] * rope_freqs(HEAD_DIM)[None, :]
    cosine = jnp.cos(angle)[:, None, :]
    sine = jnp.sin(angle)[:, None, :]
    order = jnp.arange(length)
    allowed = (segments[:, None] == segments[None, :]) & (order[:, None] >= order[None, :])
    query_full, key_full, value_full, out_full, gain_one = (
        lax.all_gather(w_query, "dp", axis=0, tiled=True),
        lax.all_gather(w_key, "dp", axis=0, tiled=True),
        lax.all_gather(w_value, "dp", axis=0, tiled=True),
        lax.all_gather(w_out, "dp", axis=0, tiled=True),
        lax.all_gather(attn_gain, "dp", axis=0, tiled=True),
    )
    gain_one = gain_one.astype(jnp.float32)
    unit_one, scale_one = norm_parts(residual)
    normed_one = (unit_one * gain_one).astype(jnp.bfloat16)
    query_rot = rotate(
        jnp.dot(normed_one, query_full, preferred_element_type=jnp.float32).reshape(
            length, -1, HEAD_DIM
        ),
        cosine,
        sine,
    ).astype(jnp.bfloat16)
    key_rot = rotate(
        jnp.dot(normed_one, key_full, preferred_element_type=jnp.float32).reshape(
            length, -1, HEAD_DIM
        ),
        cosine,
        sine,
    ).astype(jnp.bfloat16)
    value_heads = (
        jnp.dot(normed_one, value_full, preferred_element_type=jnp.float32)
        .astype(jnp.bfloat16)
        .reshape(length, -1, HEAD_DIM)
    )
    kv_local = key_rot.shape[1]
    query_group = query_rot.reshape(length, kv_local, group, HEAD_DIM)
    scores = jnp.where(
        allowed,
        jnp.einsum("qhgd,khd->hgqk", query_group, key_rot, preferred_element_type=jnp.float32)
        * factor,
        masked_score,
    )
    top = jnp.max(scores, axis=-1, keepdims=True)
    expo = jnp.exp(scores - top)
    total = jnp.sum(expo, axis=-1, keepdims=True)
    log_total = top + jnp.log(total)
    weights_low = (expo / total).astype(jnp.bfloat16)
    attended = (
        jnp.einsum("hgqk,khd->qhgd", weights_low, value_heads, preferred_element_type=jnp.float32)
        .astype(jnp.bfloat16)
        .reshape(length, -1)
    )
    attn_out = lax.psum(dot_last(attended, out_full), "tensor")
    middle = residual + attn_out
    gate_full, up_full, down_full, gain_two = (
        lax.all_gather(w_gate, "dp", axis=0, tiled=True),
        lax.all_gather(w_up, "dp", axis=0, tiled=True),
        lax.all_gather(w_down, "dp", axis=0, tiled=True),
        lax.all_gather(mlp_gain, "dp", axis=0, tiled=True),
    )
    gain_two = gain_two.astype(jnp.float32)
    unit_two, scale_two = norm_parts(middle)
    normed_two = (unit_two * gain_two).astype(jnp.bfloat16)
    gate = jnp.dot(normed_two, gate_full, preferred_element_type=jnp.float32)
    upward = jnp.dot(normed_two, up_full, preferred_element_type=jnp.float32)
    sigma = jax.nn.sigmoid(gate)
    active = (gate * sigma * upward).astype(jnp.bfloat16)
    mlp_out = lax.psum(dot_last(active, down_full).astype(jnp.bfloat16), "tensor").astype(
        jnp.float32
    )
    output = (middle + mlp_out).astype(jnp.bfloat16)
    gate_back, up_back, down_back, gain_back = (
        lax.all_gather(w_gate, "dp", axis=0, tiled=True),
        lax.all_gather(w_up, "dp", axis=0, tiled=True),
        lax.all_gather(w_down, "dp", axis=0, tiled=True),
        lax.all_gather(mlp_gain, "dp", axis=0, tiled=True),
    )
    gain_back = gain_back.astype(jnp.float32)
    down_grad = dot_first(out_grad, active)
    active_grad = jnp.dot(out_grad, down_back, preferred_element_type=jnp.float32)
    gate_delta = (active_grad * upward * sigma * (1.0 + gate * (1.0 - sigma))).astype(jnp.bfloat16)
    up_delta = (active_grad * gate * sigma).astype(jnp.bfloat16)
    gate_grad = dot_first(normed_two, gate_delta)
    up_grad = dot_first(normed_two, up_delta)
    normed_two_grad = lax.psum(
        dot_last(gate_delta, gate_back) + dot_last(up_delta, up_back), "tensor"
    )
    middle_part, mlp_gain_grad = norm_back(normed_two_grad, unit_two, scale_two, gain_back)
    middle_grad = out_grad.astype(jnp.float32) + middle_part
    query_back, key_back, value_back, out_back, gain_first = (
        lax.all_gather(w_query, "dp", axis=0, tiled=True),
        lax.all_gather(w_key, "dp", axis=0, tiled=True),
        lax.all_gather(w_value, "dp", axis=0, tiled=True),
        lax.all_gather(w_out, "dp", axis=0, tiled=True),
        lax.all_gather(attn_gain, "dp", axis=0, tiled=True),
    )
    gain_first = gain_first.astype(jnp.float32)
    attn_delta = middle_grad.astype(jnp.bfloat16)
    out_proj_grad = dot_first(attn_delta, attended)
    head_delta = (
        jnp.dot(attn_delta, out_back, preferred_element_type=jnp.float32)
        .astype(jnp.bfloat16)
        .reshape(length, kv_local, group, HEAD_DIM)
    )
    rescored = jnp.where(
        allowed,
        jnp.einsum("qhgd,khd->hgqk", query_group, key_rot, preferred_element_type=jnp.float32)
        * factor,
        masked_score,
    )
    probs = jnp.exp(rescored - log_total)
    prob_grad = jnp.einsum(
        "qhgd,khd->hgqk", head_delta, value_heads, preferred_element_type=jnp.float32
    )
    row_total = jnp.sum(probs * prob_grad, axis=-1, keepdims=True)
    score_delta = (probs * (prob_grad - row_total)).astype(jnp.bfloat16)
    query_rot_grad = (
        jnp.einsum("hgqk,khd->qhgd", score_delta, key_rot, preferred_element_type=jnp.float32)
        * factor
    )
    key_rot_grad = (
        jnp.einsum("hgqk,qhgd->khd", score_delta, query_group, preferred_element_type=jnp.float32)
        * factor
    )
    value_delta = (
        jnp.einsum(
            "hgqk,qhgd->khd",
            probs.astype(jnp.bfloat16),
            head_delta,
            preferred_element_type=jnp.float32,
        )
        .astype(jnp.bfloat16)
        .reshape(length, -1)
    )
    query_delta = (
        rotate(query_rot_grad.reshape(length, -1, HEAD_DIM), cosine, -sine)
        .astype(jnp.bfloat16)
        .reshape(length, -1)
    )
    key_delta = rotate(key_rot_grad, cosine, -sine).astype(jnp.bfloat16).reshape(length, -1)
    query_grad = dot_first(normed_one, query_delta)
    key_grad = dot_first(normed_one, key_delta)
    value_grad = dot_first(normed_one, value_delta)
    local_first = (
        dot_last(query_delta, query_back)
        + dot_last(key_delta, key_back)
        + dot_last(value_delta, value_back)
    )
    normed_one_grad = lax.psum(local_first.astype(jnp.bfloat16), "tensor").astype(jnp.float32)
    input_part, attn_gain_grad = norm_back(normed_one_grad, unit_one, scale_one, gain_first)
    input_grad = middle_grad + input_part
    (
        query_grad,
        key_grad,
        value_grad,
        out_proj_grad,
        gate_grad,
        up_grad,
        down_grad,
        attn_gain_grad,
        mlp_gain_grad,
    ) = (
        lax.psum_scatter(query_grad, "dp", scatter_dimension=0, tiled=True),
        lax.psum_scatter(key_grad, "dp", scatter_dimension=0, tiled=True),
        lax.psum_scatter(value_grad, "dp", scatter_dimension=0, tiled=True),
        lax.psum_scatter(out_proj_grad, "dp", scatter_dimension=0, tiled=True),
        lax.psum_scatter(gate_grad, "dp", scatter_dimension=0, tiled=True),
        lax.psum_scatter(up_grad, "dp", scatter_dimension=0, tiled=True),
        lax.psum_scatter(down_grad, "dp", scatter_dimension=0, tiled=True),
        lax.psum_scatter(attn_gain_grad, "dp", scatter_dimension=0, tiled=True),
        lax.psum_scatter(mlp_gain_grad, "dp", scatter_dimension=0, tiled=True),
    )
    return (
        output,
        input_grad,
        query_grad,
        key_grad,
        value_grad,
        out_proj_grad,
        gate_grad,
        up_grad,
        down_grad,
        attn_gain_grad,
        mlp_gain_grad,
    )


def solution(mesh):
    in_specs = (
        P("dp", None),
        P("dp"),
        P("dp"),
        P("dp", "tensor"),
        P("dp", "tensor"),
        P("dp", "tensor"),
        P("dp", "tensor"),
        P("dp", "tensor"),
        P("dp", "tensor"),
        P("dp", "tensor"),
        P("dp"),
        P("dp"),
        P("dp", None),
    )
    out_specs = (
        P("dp", None),
        P("dp", None),
        P("dp", "tensor"),
        P("dp", "tensor"),
        P("dp", "tensor"),
        P("dp", "tensor"),
        P("dp", "tensor"),
        P("dp", "tensor"),
        P("dp", "tensor"),
        P("dp"),
        P("dp"),
    )
    return jax.shard_map(
        on_device, mesh=mesh, in_specs=in_specs, out_specs=out_specs, check_vma=False
    )
```

profile of v0, /device:TPU:0, one launch (start us, length us, event | category | flops | bytes accessed | tf_op | source)
XLA Modules:
  0.0 2104.6 jit_solution(7362402371754869214)
XLA Ops:
  7.2 0.7 all-gather.10.cloned.1.call-update
  8.0 0.7 all-gather.12.cloned.1.call-update
  8.7 0.7 all-gather.14.cloned.1.call-update
  9.5 0.5 all-gather.16.cloned.1.call-update
  10.0 0.7 convert_element_type.94
  10.7 23.3 %all-gather = bf16[16,1,128]{2,1,0:T(2,128)(2,1)S(1)} all-gather(bf16[1,1,128]{2,1,0:T(2,128)(2,1)} %bitcast.134), channel_id=1, replica_groups=mesh['dp'=16,'tensor'=2] {'dp'}, dimensions={0}, use_global_device_ids=true | all-gather | bytes 4352 | tf_op jit(solution)/shard_map/all_gather | solution.py:87
  34.0 1.2 fusion.17
  35.2 0.8 fusion.25
  36.2 14.6 all-gather.10.cloned.1.call-done
  50.8 1.7 convolution_convert_fusion.3
  52.6 37.1 %all-gather.12.cloned.1.call-done = bf16[2048,256]{1,0:T(8,128)(2,1)} async-done(((bf16[128,256]{1,0:T(8,128)(2,1)}), bf16[2048,256]{1,0:T(8,128)(2,1)}) %all-gather.12.cloned.1.call-update) | async-done | bytes 1048592 | tf_op jit(solution)/shard_map/all_gather | solution.py:84
  89.8 2.0 fusion.38
  91.8 49.5 %all-gather.14.cloned.1.call-done = bf16[2048,1024]{1,0:T(8,128)(2,1)} async-done(((bf16[128,1024]{1,0:T(8,128)(2,1)}), bf16[2048,1024]{1,0:T(8,128)(2,1)}) %all-gather.14.cloned.1.call-update) | async-done | bytes 4194320 | tf_op jit(solution)/shard_map/all_gather | solution.py:83
  141.3 4.0 fusion.36
  145.4 0.6 copy-done.9
  147.0 45.3 %all-gather.16.cloned.1.call-done = bf16[2048,1024]{1,0:T(8,128)(2,1)} async-done(((bf16[128,1024]{1,0:T(8,128)(2,1)}), bf16[2048,1024]{1,0:T(8,128)(2,1)}) %all-gather.16.cloned.1.call-update) | async-done | bytes 4194320 | tf_op jit(solution)/shard_map/all_gather | solution.py:86
  192.3 4.7 fusion.42
  197.1 0.5 all-gather.20.cloned.1.call-update
  197.6 0.7 all-gather.18.cloned.1.call-update
  198.4 0.7 all-gather.22.cloned.1.call-update
  199.1 19.5 all-gather.1
  218.6 17.2 all-reduce.8.cloned.1.call-done
  235.8 1.4 multiply_reduce_fusion.3
  237.4 126.8 %all-gather.20.cloned.1.call-done = bf16[2048,4096]{1,0:T(8,128)(2,1)} async-done(((bf16[128,4096]{1,0:T(8,128)(2,1)}), bf16[2048,4096]{1,0:T(8,128)(2,1)}) %all-gather.20.cloned.1.call-update) | async-done | bytes 16777232 | tf_op jit(solution)/shard_map/all_gather | solution.py:133
  364.3 9.4 fusion.44
  373.7 117.4 %all-gather.18.cloned.1.call-done = bf16[2048,4096]{1,0:T(8,128)(2,1)} async-done(((bf16[128,4096]{1,0:T(8,128)(2,1)}), bf16[2048,4096]{1,0:T(8,128)(2,1)}) %all-gather.18.cloned.1.call-update) | async-done | bytes 16777232 | tf_op jit(solution)/shard_map/all_gather | solution.py:132
  491.1 9.4 fusion.43
  500.5 117.4 %all-gather.22.cloned.1.call-done = bf16[2048,4096]{1,0:T(8,128)(2,1)} async-done(((bf16[128,4096]{1,0:T(8,128)(2,1)}), bf16[2048,4096]{1,0:T(8,128)(2,1)}) %all-gather.22.cloned.1.call-update) | async-done | bytes 16777232 | tf_op jit(solution)/shard_map/all_gather | solution.py:134
  617.9 11.9 multiply_convert_fusion
  629.8 13.2 fusion.45
  643.0 12.9 convolution_add_fusion.1
  656.0 12.5 convolution_convert_fusion
  668.6 25.8 %all-reduce.10.cloned.1.call-done = f32[128,2048]{1,0:T(8,128)} async-done(((f32[128,2048]{1,0:T(8,128)}), f32[128,2048]{1,0:T(8,128)}) %all-reduce.10.cloned.1.call-update) | async-done | bytes 1048592 | tf_op jit(solution)/shard_map/psum | solution.py:161
  694.4 1.7 multiply_reduce_fusion
  696.1 1.7 multiply_add_fusion
  697.8 1.5 convolution_convert_fusion.2
  699.3 1.1 copy.55
  700.5 1.6 fusion.11
  702.1 1.7 multiply_reduce_fusion.1
  705.8 0.6 copy-done.1
  706.4 2.4 fusion.1
  709.1 17.1 convolution_bitcast_fusion
  726.3 2.5 fusion.32
  728.8 2.5 fusion.30
  731.4 5.5 fusion.22
  737.0 0.6 copy-done.19
  737.5 4.7 fusion.34
  742.3 14.3 fusion.49
  757.0 21.0 fusion.48
  778.0 0.6 copy-done.21
  778.6 0.6 dynamic-slice
  779.9 1.6 fusion.16
  781.5 63.1 %all-reduce.2 = (f32[2048]{0:T(1024)S(1)}, f32[2048]{0:T(1024)S(1)}) all-reduce(f32[2048]{0:T(1024)S(1)} %get-tuple-element.46, f32[2048]{0:T(1024)S(1)} %get-tuple-element.44), channel_id=9, replica_groups=mesh['dp'=16,'tensor'=2] {'dp'}, use_global_device_ids=true, to_apply=%region_19.20.clone | all-reduce | flops 4096 | bytes 32768
  844.6 0.6 dynamic-slice.1
  845.2 0.6 dynamic-slice.3
  845.8 2.8 fusion.13
  848.6 235.4 %reduce-scatter.20.cloned.1.call-done = f32[128,4096]{0,1:T(8,128)} async-done(((f32[2048,4096]{0,1:T(8,128)}), f32[128,4096]{0,1:T(8,128)}) %reduce-scatter.20.cloned.1.call-update) | async-done | bytes 2097168 | tf_op jit(solution)/shard_map/reduce_scatter | solution.py:245
  1083.9 2.9 copy.59
  1086.8 62.2 %reduce-scatter.10.cloned.1.call-done = f32[128,256]{1,0:T(8,128)} async-done(((f32[2048,256]{1,0:T(8,128)}), f32[128,256]{1,0:T(8,128)}) %reduce-scatter.10.cloned.1.call-update) | async-done | bytes 131088 | tf_op jit(solution)/shard_map/reduce_scatter | solution.py:240
  1149.0 65.0 %reduce-scatter.12.cloned.1.call-done = f32[128,256]{1,0:T(8,128)} async-done(((f32[2048,256]{1,0:T(8,128)}), f32[128,256]{1,0:T(8,128)}) %reduce-scatter.12.cloned.1.call-update) | async-done | bytes 131088 | tf_op jit(solution)/shard_map/reduce_scatter | solution.py:241
  1214.1 106.9 %reduce-scatter.14.cloned.1.call-done = f32[128,1024]{1,0:T(8,128)} async-done(((f32[2048,1024]{1,0:T(8,128)}), f32[128,1024]{1,0:T(8,128)}) %reduce-scatter.14.cloned.1.call-update) | async-done | bytes 524304 | tf_op jit(solution)/shard_map/reduce_scatter | solution.py:242
  1321.0 107.6 %reduce-scatter.8.cloned.1.call-done = f32[128,1024]{1,0:T(8,128)} async-done(((f32[2048,1024]{1,0:T(8,128)}), f32[128,1024]{1,0:T(8,128)}) %reduce-scatter.8.cloned.1.call-update) | async-done | bytes 524304 | tf_op jit(solution)/shard_map/reduce_scatter | solution.py:239
  1428.6 334.9 %reduce-scatter.18.cloned.1.call-done = f32[128,4096]{1,0:T(8,128)} async-done(((f32[2048,4096]{1,0:T(8,128)}), f32[128,4096]{1,0:T(8,128)}) %reduce-scatter.18.cloned.1.call-update) | async-done | bytes 2097168 | tf_op jit(solution)/shard_map/reduce_scatter | solution.py:244
  1763.5 334.3 %reduce-scatter.16.cloned.1.call-done = f32[128,4096]{1,0:T(8,128)} async-done(((f32[2048,4096]{1,0:T(8,128)}), f32[128,4096]{1,0:T(8,128)}) %reduce-scatter.16.cloned.1.call-update) | async-done | bytes 2097168 | tf_op jit(solution)/shard_map/reduce_scatter | solution.py:243
  (93 shorter events, 4.7 us)
Async XLA Ops:
  7.2 134.1 %copy-start = (bf16[128,2048]{1,0:T(8,128)(2,1)S(1)}, bf16[128,2048]{1,0:T(8,128)(2,1)}, u32[]{:S(2)}) copy-start(bf16[128,2048]{1,0:T(8,128)(2,1)} %param.13) | copy-start | bytes 1572868
  7.2 43.6 %all-gather.10.cloned.1.call-start = ((), (), s32[]{:S(2)}) async-start(), calls=%async_computation.7 | async-start | bytes 1114112 | tf_op jit(solution)/shard_map/all_gather | solution.py:85
  7.9 81.8 %all-gather.12.cloned.1.call-start = ((), (), s32[]{:S(2)}) async-start(), calls=%async_computation.8 | async-start | bytes 1114112 | tf_op jit(solution)/shard_map/all_gather | solution.py:84
  8.7 132.6 %all-gather.14.cloned.1.call-start = ((), (), s32[]{:S(2)}) async-start(), calls=%async_computation.9 | async-start | bytes 4456448 | tf_op jit(solution)/shard_map/all_gather | solution.py:83
  9.4 182.9 %all-gather.16.cloned.1.call-start = ((), (), s32[]{:S(2)}) async-start(), calls=%async_computation.10 | async-start | bytes 4456448 | tf_op jit(solution)/shard_map/all_gather | solution.py:86
  10.0 225.8 %all-reduce.8.cloned.1.call-start = ((), (), s32[]{:S(2)}) async-start(), calls=%async_computation.11 | async-start | bytes 2097152 | tf_op jit(solution)/shard_map/psum | solution.py:129
  35.2 110.1 %copy-start.18 = (f32[128]{0:T(128)}, f32[128]{0:T(128)S(1)}, u32[]{:S(2)}) copy-start(f32[128]{0:T(128)S(1)} %add_rsqrt_fusion.1) | copy-start | bytes 1540
  52.6 94.0 %copy-start.13 = (bf16[128,256]{0,1:T(8,128)(2,1)}, bf16[128,256]{0,1:T(8,128)(2,1)S(1)}, u32[]{:S(2)}) copy-start(bf16[128,256]{0,1:T(8,128)(2,1)S(1)} %copy.51) | copy-start | bytes 196612
  91.8 54.9 %copy-start.14 = (bf16[128,4,32]{0,2,1:T(8,128)(2,1)}, bf16[128,4,32]{0,2,1:T(8,128)(2,1)S(1)}, u32[]{:S(2)}) copy-start(bf16[128,4,32]{0,2,1:T(8,128)(2,1)S(1)} %get-tuple-element.63) | copy-start | bytes 98308
  91.8 54.8 %copy-start.16 = (bf16[128,4,32]{0,2,1:T(8,128)(2,1)}, bf16[128,4,32]{0,2,1:T(8,128)(2,1)S(1)}, u32[]{:S(2)}) copy-start(bf16[128,4,32]{0,2,1:T(8,128)(2,1)S(1)} %get-tuple-element.64) | copy-start | bytes 98308
  145.4 0.7 copy-start.9
  145.4 1.0 copy-start.11
  146.4 50.6 %copy-start.2 = (f32[4,4,128,128]{2,3,1,0:T(8,128)}, f32[4,4,128,128]{2,3,1,0:T(8,128)S(1)}, u32[]{:S(2)}) copy-start(f32[4,4,128,128]{2,3,1,0:T(8,128)S(1)} %get-tuple-element.69) | copy-start | bytes 3145732
  147.0 51.4 %copy-start.6 = (bf16[4,64,4,128]{3,1,2,0:T(8,128)(2,1)}, bf16[4,64,4,128]{3,1,2,0:T(8,128)(2,1)S(1)}, u32[]{:S(2)}) copy-start(bf16[4,64,4,128]{3,1,2,0:T(8,128)(2,1)S(1)} %convolution_convert_fusion.1) | copy-start | bytes 786436
  192.3 6.9 copy-start.20
  197.0 167.3 %all-gather.20.cloned.1.call-start = ((), (), s32[]{:S(2)}) async-start(), calls=%async_computation.13 | async-start | bytes 17825792 | tf_op jit(solution)/shard_map/all_gather | solution.py:133
  197.6 293.5 %all-gather.18.cloned.1.call-start = ((), (), s32[]{:S(2)}) async-start(), calls=%async_computation.12 | async-start | bytes 17825792 | tf_op jit(solution)/shard_map/all_gather | solution.py:132
  198.3 419.5 %all-gather.22.cloned.1.call-start = ((), (), s32[]{:S(2)}) async-start(), calls=%async_computation.14 | async-start | bytes 17825792 | tf_op jit(solution)/shard_map/all_gather | solution.py:134
  199.1 495.3 %all-reduce.10.cloned.1.call-start = ((), (), s32[]{:S(2)}) async-start(), calls=%async_computation.15 | async-start | bytes 2097152 | tf_op jit(solution)/shard_map/psum | solution.py:161
  629.8 26.3 %copy-start.5 = (bf16[128,4096]{1,0:T(8,128)(2,1)}, bf16[128,4096]{1,0:T(8,128)(2,1)S(1)}, u32[]{:S(2)}) copy-start(bf16[128,4096]{1,0:T(8,128)(2,1)S(1)} %get-tuple-element.56) | copy-start | bytes 3145732
  655.9 123.9 %all-reduce.12.cloned.1.call-start = ((), (), s32[]{:S(2)}) async-start(), calls=%async_computation.23 | async-start | bytes 2097152 | tf_op jit(solution)/shard_map/psum | solution.py:144
  694.4 3.4 copy-start.4
  700.4 3.4 copy-start.3
  700.4 3.7 copy-start.10
  700.4 3.7 copy-start.12
  700.5 4.0 copy-start.15
  700.5 4.0 copy-start.17
  702.1 2.7 copy-start.7
  703.9 1.5 copy-start.8
  704.1 2.3 copy-start.1
  708.8 375.1 %reduce-scatter.20.cloned.1.call-start = ((), (), s32[]{:S(2)}) async-start(), calls=%async_computation.22 | async-start | bytes 35651584 | tf_op jit(solution)/shard_map/reduce_scatter | solution.py:245
  726.2 422.8 %reduce-scatter.10.cloned.1.call-start = ((), (), s32[]{:S(2)}) async-start(), calls=%async_computation.17 | async-start | bytes 2228224 | tf_op jit(solution)/shard_map/reduce_scatter | solution.py:240
  728.8 485.3 %reduce-scatter.12.cloned.1.call-start = ((), (), s32[]{:S(2)}) async-start(), calls=%async_computation.18 | async-start | bytes 2228224 | tf_op jit(solution)/shard_map/reduce_scatter | solution.py:241
  731.4 589.6 %reduce-scatter.14.cloned.1.call-start = ((), (), s32[]{:S(2)}) async-start(), calls=%async_computation.19 | async-start | bytes 8912896 | tf_op jit(solution)/shard_map/reduce_scatter | solution.py:242
  736.9 0.7 copy-start.19
  736.9 691.7 %reduce-scatter.8.cloned.1.call-start = ((), (), s32[]{:S(2)}) async-start(), calls=%async_computation.16 | async-start | bytes 8912896 | tf_op jit(solution)/shard_map/reduce_scatter | solution.py:239
  742.2 1021.3 %reduce-scatter.18.cloned.1.call-start = ((), (), s32[]{:S(2)}) async-start(), calls=%async_computation.21 | async-start | bytes 35651584 | tf_op jit(solution)/shard_map/reduce_scatter | solution.py:244
  756.7 1341.2 %reduce-scatter.16.cloned.1.call-start = ((), (), s32[]{:S(2)}) async-start(), calls=%async_computation.20 | async-start | bytes 35651584 | tf_op jit(solution)/shard_map/reduce_scatter | solution.py:243
  777.9 0.7 copy-start.21
Sparse Core Ops, SparseCore 0:
  10.2 40.5 all-gather.9
  52.9 36.7 all-gather.11
  91.9 49.3 all-gather.13
  143.3 48.8 all-gather.15
  197.1 38.6 all-reduce.7
  237.8 126.4 all-gather.19
  366.4 124.5 all-gather.17
  493.2 124.5 all-gather.21
  656.1 38.2 all-reduce.9
  708.9 40.0 all-reduce.11
  753.3 330.5 reduce-scatter.19
  1088.1 60.8 reduce-scatter.9
  1153.3 60.6 reduce-scatter.11
  1218.6 102.3 reduce-scatter.13
  1325.5 103.0 reduce-scatter.7
  1433.3 330.1 reduce-scatter.17
  1768.2 329.6 reduce-scatter.15
where the time goes:
time: 2110 us; the launch traced here: 2100 us
  waiting for transfers between devices  1800 us (85%)
  matrix products  159 us (8%)
  blocking collectives  106 us (5%)
    reduce_scatter x1, waiting for transfers between devices, on_device(): lax.psum_scatter(up_grad, 'dp', scatter_dimension=0, tiled=True)  335 us
    reduce_scatter x1, waiting for transfers between devices, on_device(): lax.psum_scatter(gate_grad, 'dp', scatter_dimension=0, tiled=True)  334 us
    reduce_scatter x1, waiting for transfers between devices, on_device(): lax.psum_scatter(down_grad, 'dp', scatter_dimension=0, tiled=True)  235 us
    all_gather x1, waiting for transfers between devices, on_device(): lax.all_gather(w_up, 'dp', axis=0, tiled=True)  127 us
    all_gather x1, waiting for transfers between devices, on_device(): lax.all_gather(w_down, 'dp', axis=0, tiled=True)  117 us
    all_gather x1, waiting for transfers between devices, on_device(): lax.all_gather(w_gate, 'dp', axis=0, tiled=True)  117 us
    reduce_scatter x1, waiting for transfers between devices, on_device(): lax.psum_scatter(query_grad, 'dp', scatter_dimension=0, tiled=True)  108 us
    reduce_scatter x1, waiting for transfers between devices, on_device(): lax.psum_scatter(out_proj_grad, 'dp', scatter_dimension=0, tiled=True)  107 us
  transfers between devices with their start and end apart: 17, of which 16 were waited for; matrix products, arithmetic and copies ran while one was open for 6% of the time, Pallas kernels for 0%

commit v1 on v0

--- a/solution.py
+++ b/solution.py
@@ -10,6 +10,19 @@
 norm_eps = 1e-05
 rope_base = 500000.0
 masked_score = -1e30
+
+
+def gather_around(value, axis, dim):
+    length, index, span = (lax.axis_size(axis), lax.axis_index(axis), value.shape[dim])
+    right = [(i, (i + 1) % length) for i in range(length)]
+    filled = jnp.zeros((*value.shape[:dim], length * span, *value.shape[dim + 1 :]), value.dtype)
+    held = value
+    for step in range(length):
+        owner = (index - step) % length
+        filled = lax.dynamic_update_slice_in_dim(filled, held, owner * span, axis=dim)
+        if step < length - 1:
+            held = lax.ppermute(held, axis, right)
+    return filled
 
 
 def rope_freqs(head_dim):
@@ -83,7 +96,7 @@
         lax.all_gather(w_query, "dp", axis=0, tiled=True),
         lax.all_gather(w_key, "dp", axis=0, tiled=True),
         lax.all_gather(w_value, "dp", axis=0, tiled=True),
-        lax.all_gather(w_out, "dp", axis=0, tiled=True),
+        gather_around(w_out, "dp", 0),
         lax.all_gather(attn_gain, "dp", axis=0, tiled=True),
     )
     gain_one = gain_one.astype(jnp.float32)

time: 2110 us -> 2140 us (1.014)
  waiting for transfers between devices: 1800 us -> 1830 us
    ppermute x0 -> x15, waiting for transfers between devices: none -> 119 us  [gather_around(): held = lax.ppermute(held, axis, right)]
    all_gather x1, waiting for transfers between devices: 49.5 us -> 0.01 us  [on_device(): lax.all_gather(w_query, 'dp', axis=0, tiled=True)]
    all_gather x1, waiting for transfers between devices: 37.1 us -> 0.01 us  [on_device(): lax.all_gather(w_key, 'dp', axis=0, tiled=True)]
  transfers between devices with their start and end apart: 17 -> 32, of which waited for: 16 -> 27; matrix products, arithmetic and copies ran while one was open for 6% -> 6% of each run, Pallas kernels for 0% -> 0%
where the time goes in v1:
time: 2140 us
  waiting for transfers between devices  1830 us (86%)
  matrix products  157 us (7%)
  blocking collectives  96.4 us (5%)
  local copies, waits for them, and re-layouts  24.8 us (1%)
    reduce_scatter x1, waiting for transfers between devices, on_device(): lax.psum_scatter(up_grad, 'dp', scatter_dimension=0, tiled=True)  335 us
    reduce_scatter x1, waiting for transfers between devices, on_device(): lax.psum_scatter(gate_grad, 'dp', scatter_dimension=0, tiled=True)  334 us
    reduce_scatter x1, waiting for transfers between devices, on_device(): lax.psum_scatter(down_grad, 'dp', scatter_dimension=0, tiled=True)  238 us
    all_gather x1, waiting for transfers between devices, on_device(): lax.all_gather(w_gate, 'dp', axis=0, tiled=True)  127 us
    ppermute x15, waiting for transfers between devices, gather_around(): held = lax.ppermute(held, axis, right)  119 us
    all_gather x1, waiting for transfers between devices, on_device(): lax.all_gather(w_down, 'dp', axis=0, tiled=True)  117 us
    all_gather x1, waiting for transfers between devices, on_device(): lax.all_gather(w_up, 'dp', axis=0, tiled=True)  117 us
    reduce_scatter x1, waiting for transfers between devices, on_device(): lax.psum_scatter(out_proj_grad, 'dp', scatter_dimension=0, tiled=True)  108 us
  transfers between devices with their start and end apart: 32, of which 27 were waited for; matrix products, arithmetic and copies ran while one was open for 6% of the time, Pallas kernels for 0%

profile of v1, /device:TPU:0, one launch (start us, length us, event | category | flops | bytes accessed | tf_op | source)
XLA Modules:
  0.0 2136.8 jit_solution(2617676982825267050)
XLA Ops:
  10.0 9.2 collective-permute-done
  19.2 9.4 collective-permute-done.1
  28.6 8.5 collective-permute-done.2
  37.1 11.1 collective-permute-done.3
  48.2 8.5 collective-permute-done.4
  56.7 1.2 fusion.17
  57.9 0.8 fusion.25
  58.8 6.5 collective-permute-done.5
  66.7 7.5 collective-permute-done.6
  74.5 17.9 all-gather
  92.5 2.5 broadcast_in_dim.12
  98.0 0.8 constant_dynamic-update-slice_fusion.11
  98.8 6.2 collective-permute-done.8
  107.1 11.4 collective-permute-done.9
  118.6 1.6 convolution_convert_fusion.3
  120.3 7.0 collective-permute-done.10
  127.3 1.8 fusion.38
  129.1 11.4 collective-permute-done.11
  141.3 9.7 collective-permute-done.12
  153.2 6.3 collective-permute-done.13
  161.7 6.3 collective-permute-done.14
  168.7 4.0 fusion.36
  174.0 0.8 copy-done.2
  175.8 4.7 fusion.42
  182.5 17.7 all-gather.1
  200.2 17.8 all-reduce.8.cloned.1.call-done
  218.1 1.4 multiply_reduce_fusion.3
  219.7 126.8 %all-gather.16.cloned.1.call-done = bf16[2048,4096]{1,0:T(8,128)(2,1)} async-done(((bf16[128,4096]{1,0:T(8,128)(2,1)}), bf16[2048,4096]{1,0:T(8,128)(2,1)}) %all-gather.16.cloned.1.call-update) | async-done | bytes 16777232 | tf_op jit(solution)/shard_map/all_gather | solution.py:145
  346.5 9.4 fusion.43
  356.0 117.2 %all-gather.18.cloned.1.call-done = bf16[2048,4096]{1,0:T(8,128)(2,1)} async-done(((bf16[128,4096]{1,0:T(8,128)(2,1)}), bf16[2048,4096]{1,0:T(8,128)(2,1)}) %all-gather.18.cloned.1.call-update) | async-done | bytes 16777232 | tf_op jit(solution)/shard_map/all_gather | solution.py:146
  473.2 9.4 fusion.44
  482.6 117.4 %all-gather.20.cloned.1.call-done = bf16[2048,4096]{1,0:T(8,128)(2,1)} async-done(((bf16[128,4096]{1,0:T(8,128)(2,1)}), bf16[2048,4096]{1,0:T(8,128)(2,1)}) %all-gather.20.cloned.1.call-update) | async-done | bytes 16777232 | tf_op jit(solution)/shard_map/all_gather | solution.py:147
  600.0 11.9 multiply_convert_fusion
  611.9 13.2 fusion.45
  625.1 12.9 convolution_add_fusion.1
  638.9 12.5 convolution_convert_fusion
  651.4 25.1 %all-reduce.10.cloned.1.call-done = f32[128,2048]{1,0:T(8,128)} async-done(((f32[128,2048]{1,0:T(8,128)}), f32[128,2048]{1,0:T(8,128)}) %all-reduce.10.cloned.1.call-update) | async-done | bytes 1048592 | tf_op jit(solution)/shard_map/psum | solution.py:174
  676.5 2.2 multiply_reduce_fusion
  678.7 1.7 multiply_add_fusion
  680.4 48.7 %all-gather.22.cloned.1.call-done = bf16[2048,1024]{1,0:T(8,128)(2,1)} async-done(((bf16[128,1024]{1,0:T(8,128)(2,1)}), bf16[2048,1024]{1,0:T(8,128)(2,1)}) %all-gather.22.cloned.1.call-update) | async-done | bytes 4194320 | tf_op jit(solution)/shard_map/all_gather | solution.py:183
  729.1 3.6 convolution_convert_fusion.2
  732.7 1.1 copy.55
  733.9 1.7 multiply_reduce_fusion.1
  735.6 1.6 multiply_convert_fusion.3
  739.8 2.3 fusion.1
  742.4 17.1 convolution_bitcast_fusion
  760.2 1.9 fusion.32
  762.1 1.9 fusion.30
  764.0 4.7 fusion.34
  768.8 0.9 copy-done.6
  769.7 4.5 fusion.22
  774.3 14.4 fusion.49
  789.0 21.0 fusion.48
  811.9 1.5 fusion.16
  813.4 60.9 %all-reduce.2 = (f32[2048]{0:T(1024)S(1)}, f32[2048]{0:T(1024)S(1)}) all-reduce(f32[2048]{0:T(1024)S(1)} %get-tuple-element.46, f32[2048]{0:T(1024)S(1)} %copy-done.20), channel_id=9, replica_groups=mesh['dp'=16,'tensor'=2] {'dp'}, use_global_device_ids=true, to_apply=%region_19.20.clone | all-reduce | flops 4096 | bytes 32768
  875.5 2.8 fusion.13
  878.3 237.9 %reduce-scatter.20.cloned.1.call-done = f32[128,4096]{0,1:T(8,128)} async-done(((f32[2048,4096]{0,1:T(8,128)}), f32[128,4096]{0,1:T(8,128)}) %reduce-scatter.20.cloned.1.call-update) | async-done | bytes 2097168 | tf_op jit(solution)/shard_map/reduce_scatter | solution.py:258
  1116.1 2.9 copy.59
  1119.0 62.2 %reduce-scatter.10.cloned.1.call-done = f32[128,256]{1,0:T(8,128)} async-done(((f32[2048,256]{1,0:T(8,128)}), f32[128,256]{1,0:T(8,128)}) %reduce-scatter.10.cloned.1.call-update) | async-done | bytes 131088 | tf_op jit(solution)/shard_map/reduce_scatter | solution.py:253
  1181.2 65.1 %reduce-scatter.12.cloned.1.call-done = f32[128,256]{1,0:T(8,128)} async-done(((f32[2048,256]{1,0:T(8,128)}), f32[128,256]{1,0:T(8,128)}) %reduce-scatter.12.cloned.1.call-update) | async-done | bytes 131088 | tf_op jit(solution)/shard_map/reduce_scatter | solution.py:254
  1246.3 106.9 %reduce-scatter.8.cloned.1.call-done = f32[128,1024]{1,0:T(8,128)} async-done(((f32[2048,1024]{1,0:T(8,128)}), f32[128,1024]{1,0:T(8,128)}) %reduce-scatter.8.cloned.1.call-update) | async-done | bytes 524304 | tf_op jit(solution)/shard_map/reduce_scatter | solution.py:252
  1353.2 107.6 %reduce-scatter.14.cloned.1.call-done = f32[128,1024]{1,0:T(8,128)} async-done(((f32[2048,1024]{1,0:T(8,128)}), f32[128,1024]{1,0:T(8,128)}) %reduce-scatter.14.cloned.1.call-update) | async-done | bytes 524304 | tf_op jit(solution)/shard_map/reduce_scatter | solution.py:255
  1460.8 334.9 %reduce-scatter.18.cloned.1.call-done = f32[128,4096]{1,0:T(8,128)} async-done(((f32[2048,4096]{1,0:T(8,128)}), f32[128,4096]{1,0:T(8,128)}) %reduce-scatter.18.cloned.1.call-update) | async-done | bytes 2097168 | tf_op jit(solution)/shard_map/reduce_scatter | solution.py:257
  1795.7 334.3 %reduce-scatter.16.cloned.1.call-done = f32[128,4096]{1,0:T(8,128)} async-done(((f32[2048,4096]{1,0:T(8,128)}), f32[128,4096]{1,0:T(8,128)}) %reduce-scatter.16.cloned.1.call-update) | async-done | bytes 2097168 | tf_op jit(solution)/shard_map/reduce_scatter | solution.py:256
  (146 shorter events, 27.0 us)
Async XLA Ops:
  7.2 87.8 %copy-start.7 = (bf16[128,1024]{1,0:T(8,128)(2,1)S(1)}, bf16[128,1024]{1,0:T(8,128)(2,1)}, u32[]{:S(2)}) copy-start(bf16[128,1024]{1,0:T(8,128)(2,1)} %param.19) | copy-start | bytes 786436
  7.2 111.4 %all-gather.10.cloned.1.call-start = ((), (), s32[]{:S(2)}) async-start(), calls=%async_computation.7 | async-start | bytes 1114112 | tf_op jit(solution)/shard_map/all_gather | solution.py:98
  7.9 119.3 %all-gather.12.cloned.1.call-start = ((), (), s32[]{:S(2)}) async-start(), calls=%async_computation.8 | async-start | bytes 1114112 | tf_op jit(solution)/shard_map/all_gather | solution.py:97
  8.7 160.1 %all-gather.14.cloned.1.call-start = ((), (), s32[]{:S(2)}) async-start(), calls=%async_computation.9 | async-start | bytes 4456448 | tf_op jit(solution)/shard_map/all_gather | solution.py:96
  9.4 208.7 %all-reduce.8.cloned.1.call-start = ((), (), s32[]{:S(2)}) async-start(), calls=%async_computation.10 | async-start | bytes 2097152 | tf_op jit(solution)/shard_map/psum | solution.py:142
  9.5 9.8 collective-permute-start
  19.2 9.4 collective-permute-start.1
  28.6 8.5 collective-permute-start.2
  37.1 11.1 collective-permute-start.3
  48.2 8.5 collective-permute-start.4
  56.7 8.6 collective-permute-start.5
  65.3 8.9 collective-permute-start.6
  66.7 106.0 %copy-start.12 = (f32[128,32]{0,1:T(8,128)}, f32[128,32]{0,1:T(8,128)S(1)}, u32[]{:S(2)}) copy-start(f32[128,32]{0,1:T(8,128)S(1)} %get-tuple-element.67) | copy-start | bytes 49156
  74.2 22.3 %collective-permute-start.7 = (bf16[128,1024]{1,0:T(8,128)(2,1)S(1)}, bf16[128,1024]{1,0:T(8,128)(2,1)S(1)}, u32[]{:S(2)}, u32[]{:S(2)}) collective-permute-start(bf16[128,1024]{1,0:T(8,128)(2,1)S(1)} %collective-permute-done.6), channel_id=1, source_target_pairs={{0,2},{2,4},{4,6},{6,8},{8,10},{10,12},{12,14},{14,16},{16,18},{18... | collective-permute-start | bytes 786440 | tf_op jit(solution)/shard_map/ppermute | solution.py:24
  74.2 94.6 %copy-start.21 = (f32[128]{0:T(128)}, f32[128]{0:T(128)S(1)}, u32[]{:S(2)}) copy-start(f32[128]{0:T(128)S(1)} %add_rsqrt_fusion.1) | copy-start | bytes 1540
  92.4 26.1 %copy-start = (bf16[128,2048]{1,0:T(8,128)(2,1)S(1)}, bf16[128,2048]{1,0:T(8,128)(2,1)}, u32[]{:S(2)}) copy-start(bf16[128,2048]{1,0:T(8,128)(2,1)} %param.13) | copy-start | bytes 1572868
  96.4 8.5 collective-permute-start.8
  105.0 13.6 collective-permute-start.9
  118.6 8.7 collective-permute-start.10
  120.3 53.7 %copy-start.14 = (bf16[128,256]{0,1:T(8,128)(2,1)}, bf16[128,256]{0,1:T(8,128)(2,1)S(1)}, u32[]{:S(2)}) copy-start(bf16[128,256]{0,1:T(8,128)(2,1)S(1)} %copy.51) | copy-start | bytes 196612
  127.3 13.2 collective-permute-start.11
  140.5 10.5 collective-permute-start.12
  140.5 32.3 %copy-start.16 = (bf16[128,4,32]{0,2,1:T(8,128)(2,1)}, bf16[128,4,32]{0,2,1:T(8,128)(2,1)S(1)}, u32[]{:S(2)}) copy-start(bf16[128,4,32]{0,2,1:T(8,128)(2,1)S(1)} %get-tuple-element.63) | copy-start | bytes 98308
  140.5 32.3 %copy-start.18 = (bf16[128,4,32]{0,2,1:T(8,128)(2,1)}, bf16[128,4,32]{0,2,1:T(8,128)(2,1)S(1)}, u32[]{:S(2)}) copy-start(bf16[128,4,32]{0,2,1:T(8,128)(2,1)S(1)} %get-tuple-element.64) | copy-start | bytes 98308
  151.0 8.5 collective-permute-start.13
  159.5 8.5 collective-permute-start.14
  172.8 0.7 copy-start.10
  173.8 1.0 copy-start.2
  175.1 0.7 copy-start.5
  175.8 6.7 copy-start.23
  180.6 166.0 %all-gather.16.cloned.1.call-start = ((), (), s32[]{:S(2)}) async-start(), calls=%async_computation.11 | async-start | bytes 17825792 | tf_op jit(solution)/shard_map/all_gather | solution.py:145
  181.2 292.0 %all-gather.18.cloned.1.call-start = ((), (), s32[]{:S(2)}) async-start(), calls=%async_computation.12 | async-start | bytes 17825792 | tf_op jit(solution)/shard_map/all_gather | solution.py:146
  181.7 418.2 %all-gather.20.cloned.1.call-start = ((), (), s32[]{:S(2)}) async-start(), calls=%async_computation.13 | async-start | bytes 17825792 | tf_op jit(solution)/shard_map/all_gather | solution.py:147
  182.5 494.0 %all-reduce.10.cloned.1.call-start = ((), (), s32[]{:S(2)}) async-start(), calls=%async_computation.14 | async-start | bytes 2097152 | tf_op jit(solution)/shard_map/psum | solution.py:174
  611.9 27.0 %copy-start.4 = (bf16[128,4096]{1,0:T(8,128)(2,1)}, bf16[128,4096]{1,0:T(8,128)(2,1)S(1)}, u32[]{:S(2)}) copy-start(bf16[128,4096]{1,0:T(8,128)(2,1)S(1)} %get-tuple-element.56) | copy-start | bytes 3145732
  638.1 91.0 %all-gather.22.cloned.1.call-start = ((), (), s32[]{:S(2)}) async-start(), calls=%async_computation.15 | async-start | bytes 4456448 | tf_op jit(solution)/shard_map/all_gather | solution.py:183
  638.8 173.1 %all-reduce.12.cloned.1.call-start = ((), (), s32[]{:S(2)}) async-start(), calls=%async_computation.23 | async-start | bytes 2097152 | tf_op jit(solution)/shard_map/psum | solution.py:157
  733.8 3.4 copy-start.17
  733.8 3.4 copy-start.19
  733.8 3.6 copy-start.11
  733.9 3.9 copy-start.3
  733.9 4.2 copy-start.13
  733.9 4.2 copy-start.15
  735.6 2.7 copy-start.9
  737.2 1.6 copy-start.8
  737.4 2.3 copy-start.1
  742.1 374.0 %reduce-scatter.20.cloned.1.call-start = ((), (), s32[]{:S(2)}) async-start(), calls=%async_computation.22 | async-start | bytes 35651584 | tf_op jit(solution)/shard_map/reduce_scatter | solution.py:258
  759.5 0.7 copy-start.22
  759.5 421.7 %reduce-scatter.10.cloned.1.call-start = ((), (), s32[]{:S(2)}) async-start(), calls=%async_computation.17 | async-start | bytes 2228224 | tf_op jit(solution)/shard_map/reduce_scatter | solution.py:253
  762.1 484.2 %reduce-scatter.12.cloned.1.call-start = ((), (), s32[]{:S(2)}) async-start(), calls=%async_computation.18 | async-start | bytes 2228224 | tf_op jit(solution)/shard_map/reduce_scatter | solution.py:254
  764.0 589.2 %reduce-scatter.8.cloned.1.call-start = ((), (), s32[]{:S(2)}) async-start(), calls=%async_computation.16 | async-start | bytes 8912896 | tf_op jit(solution)/shard_map/reduce_scatter | solution.py:252
  768.7 1.0 copy-start.6
  768.7 692.1 %reduce-scatter.14.cloned.1.call-start = ((), (), s32[]{:S(2)}) async-start(), calls=%async_computation.19 | async-start | bytes 8912896 | tf_op jit(solution)/shard_map/reduce_scatter | solution.py:255
  774.2 1021.5 %reduce-scatter.18.cloned.1.call-start = ((), (), s32[]{:S(2)}) async-start(), calls=%async_computation.21 | async-start | bytes 35651584 | tf_op jit(solution)/shard_map/reduce_scatter | solution.py:257
  788.7 1341.3 %reduce-scatter.16.cloned.1.call-start = ((), (), s32[]{:S(2)}) async-start(), calls=%async_computation.20 | async-start | bytes 35651584 | tf_op jit(solution)/shard_map/reduce_scatter | solution.py:256
  810.0 0.7 copy-start.24
  810.0 3.4 copy-start.20
Sparse Core Ops, SparseCore 0:
  10.2 41.8 all-gather.9
  54.2 38.9 all-gather.11
  95.4 53.7 all-gather.13
  180.7 37.3 all-reduce.7
  220.1 126.4 all-gather.15
  348.5 124.5 all-gather.17
  475.3 124.5 all-gather.19
  638.2 38.2 all-reduce.9
  678.7 50.3 all-gather.21
  742.2 38.6 all-reduce.11
  785.2 330.9 reduce-scatter.19
  1120.3 60.8 reduce-scatter.9
  1185.5 60.7 reduce-scatter.11
  1250.8 102.3 reduce-scatter.7
  1357.7 103.0 reduce-scatter.13
  1465.5 330.1 reduce-scatter.17
  1800.3 329.5 reduce-scatter.15
